TPU v7x, 256 devices: a whole 4x4x8 slice. The times are simulated.
256 devices in a mesh: crop: 2 (over y_hi), rows: 16 (over y_lo, x, core), hid: 8 (over z).
Axes of the slice: x: 4, y: 4 (y_hi: 2, y_lo: 2; y = y_hi * 2 + y_lo), z: 8, core: 2. Of those that a mesh axis runs over, the one named last changes fastest.
Arguments:
- tokens: bfloat16 [2, 32, 64, 4096], P('crop', 'rows', None, 'hid'), may hold values from -6 to 6
- cotangent: bfloat16 [2, 32, 64, 4096], P('crop', 'rows', None, 'hid'), may hold values from -6 to 6
- weight_in: bfloat16 [256, 64, 5, 256], P('rows', 'hid'), may hold values from -0.15625 to 0.15625
- weight_out: bfloat16 [256, 64, 5, 256], P('rows', 'hid'), may hold values from -0.078125 to 0.078125
- mix_kernel: float32 [9, 16384], P(None, 'hid'), may hold values from -4 to 4
- block_rows: int32 [64, 5], P('hid'), may hold values from 0 to 15, as said below
Outputs:
- grad_tokens: bfloat16 [2, 32, 64, 4096], P('crop', 'rows', None, 'hid')
- grad_w_in: float32 [256, 64, 5, 256], P(('crop', 'rows'), 'hid')
- grad_w_out: float32 [256, 64, 5, 256], P(('crop', 'rows'), 'hid')
- grad_kernel: float32 [9, 16384], P(None, 'hid')
Inputs may be any that keep to these rules, and one draw needn't show every extreme that they name: In each block column c, block_rows[c, 0] is a label L and block_rows[c, k] for k >= 1 is L with bit k - 1 flipped, so the 5 entries of a column differ; every value is the label of equally many block columns.
All inputs are finite; a program needn't handle non-finite values.
Results may differ from a plain program's by a relative error of at most 0.019.
Values may be sent and summed in bfloat16 or wider, within the bound.
No kernel may reach another device: no remote copies, remote signals or barrier semaphores. Data moves between devices by JAX's collectives and lax.ppermute only.
A program may use at most 128 MiB of HBM per device.

v0:
```python
import jax
import jax.numpy as jnp
from jax import lax
from jax.sharding import PartitionSpec as P

root_two_pi = 0.7978845608
cubic_coef = 0.044715
loss_scale = 0.03125


def padded(shard, sides, width):
    for axis, dim in sides:
        devices, length = (lax.axis_size(axis), shard.shape[dim])
        up = [(i, (i + 1) % devices) for i in range(devices - 1)]
        down = [(j, i) for i, j in up]
        last = lax.slice_in_dim(shard, length - width, length, axis=dim)
        initial = lax.slice_in_dim(shard, 0, width, axis=dim)
        before = lax.ppermute(last, axis, up)
        after = lax.ppermute(initial, axis, down)
        shard = jnp.concatenate([before, shard, after], axis=dim)
    return shard


def gelu_pair(preact):
    inner = root_two_pi * (preact + cubic_coef * preact * preact * preact)
    tanh_val = jnp.tanh(inner)
    gelu_out = 0.5 * preact * (1.0 + tanh_val)
    slopes = 0.5 * (1.0 + tanh_val) + 0.5 * preact * (1.0 - tanh_val * tanh_val) * root_two_pi * (
        1.0 + 3.0 * cubic_coef * preact * preact
    )
    return (gelu_out, slopes)


def on_device(tokens, cotangent, weight_in, weight_out, mix_kernel, block_rows):
    in_panel, out_panel = (
        lax.all_gather(weight_in, "rows", axis=0, tiled=True),
        lax.all_gather(weight_out, "rows", axis=0, tiled=True),
    )
    tok_full, cot_full = (
        lax.all_gather(tokens, "hid", axis=3, tiled=True),
        lax.all_gather(cotangent, "hid", axis=3, tiled=True),
    )
    crop_count, height, grid_width, depth_all = tok_full.shape
    tok_count = crop_count * height * grid_width
    block_size = in_panel.shape[0]
    col_count = in_panel.shape[1]
    nnz_count = in_panel.shape[2]
    block_count = depth_all // block_size
    hidden_local = col_count * block_size
    flat_rows = block_rows.reshape(-1)
    in_select = jnp.take(
        tok_full.reshape(tok_count, block_count, block_size), flat_rows, axis=1
    ).reshape(tok_count, col_count, nnz_count, block_size)
    grad_select = jnp.take(
        cot_full.reshape(tok_count, block_count, block_size), flat_rows, axis=1
    ).reshape(tok_count, col_count, nnz_count, block_size)
    pre_act = jnp.einsum("tckb,bcke->tce", in_select, in_panel, preferred_element_type=jnp.float32)
    gelu_out, slopes = gelu_pair(pre_act)
    active = gelu_out.astype(jnp.bfloat16).reshape(crop_count, height, grid_width, hidden_local)
    act_rim = padded(active, (("rows", 1),), 1)
    mix_grad = (
        jnp.einsum("tckd,fckd->tcf", grad_select, out_panel, preferred_element_type=jnp.float32)
        .astype(jnp.bfloat16)
        .reshape(crop_count, height, grid_width, hidden_local)
    )
    grad_rim = padded(mix_grad, (("rows", 1),), 1)
    act_pad = jnp.pad(act_rim.astype(jnp.float32), ((0, 0), (0, 0), (1, 1), (0, 0)))
    grad_pad = jnp.pad(grad_rim.astype(jnp.float32), ((0, 0), (0, 0), (1, 1), (0, 0)))
    grad_grid = mix_grad.astype(jnp.float32)
    mix_sum = jnp.zeros((crop_count, height, grid_width, hidden_local), jnp.float32)
    act_grad = jnp.zeros((crop_count, height, grid_width, hidden_local), jnp.float32)
    kern_terms = []
    for row_off in range(3):
        for col_off in range(3):
            tap = mix_kernel[3 * row_off + col_off]
            shifted = act_pad[:, row_off : row_off + height, col_off : col_off + grid_width]
            mix_sum = mix_sum + tap * shifted
            act_grad = (
                act_grad
                + tap
                * grad_pad[
                    :, 2 - row_off : 2 - row_off + height, 2 - col_off : 2 - col_off + grid_width
                ]
            )
            kern_terms.append(jnp.sum(shifted * grad_grid, axis=(0, 1, 2)))
    kern_local = jnp.stack(kern_terms, axis=0) * loss_scale
    mix_out = mix_sum.astype(jnp.bfloat16).reshape(tok_count, col_count, block_size)
    pre_grad = (act_grad.reshape(tok_count, col_count, block_size) * slopes).astype(jnp.bfloat16)
    kern_total = lax.psum(kern_local.astype(jnp.bfloat16), ("crop", "rows")).astype(jnp.float32)
    back_select = jnp.einsum(
        "tce,bcke->tckb", pre_grad, in_panel, preferred_element_type=jnp.float32
    )
    one_hot = (
        block_rows[:, :, None] == jnp.arange(block_count, dtype=jnp.int32)[None, None, :]
    ).astype(jnp.float32)
    token_terms = jnp.einsum(
        "tckb,ckr->trb", back_select, one_hot, precision=lax.Precision.HIGHEST
    ).reshape(crop_count, height, grid_width, depth_all)
    grad_tokens = lax.psum_scatter(
        token_terms.astype(jnp.bfloat16), "hid", scatter_dimension=3, tiled=True
    )
    first_term = jnp.einsum(
        "tckb,tce->bcke", in_select, pre_grad, preferred_element_type=jnp.float32
    )
    second_term = jnp.einsum(
        "tcf,tckd->fckd", mix_out, grad_select, preferred_element_type=jnp.float32
    )
    share_sums = lax.psum_scatter(
        (jnp.stack([first_term, second_term], axis=1) * loss_scale).astype(jnp.bfloat16),
        ("crop", "rows"),
        scatter_dimension=0,
        tiled=True,
    ).astype(jnp.float32)
    return (grad_tokens, share_sums[:, 0], share_sums[:, 1], kern_total)


def solution(mesh):
    placed = (
        P("crop", "rows", None, "hid"),
        P("crop", "rows", None, "hid"),
        P("rows", "hid", None, None),
        P("rows", "hid", None, None),
        P(None, "hid"),
        P("hid", None),
    )
    return jax.shard_map(
        on_device,
        mesh=mesh,
        in_specs=placed,
        out_specs=(
            P("crop", "rows", None, "hid"),
            P(("crop", "rows"), "hid", None, None),
            P(("crop", "rows"), "hid", None, None),
            P(None, "hid"),
        ),
        check_vma=False,
    )
```

profile of v0, /device:TPU:4, one launch (start us, length us, event | category | flops | bytes accessed | tf_op | source)
XLA Modules:
  0.0 380.4 jit_solution(11429003799002727429)
XLA Ops:
  13.2 38.3 %all-gather.9.cloned.1.call-done = bf16[1,2,64,4096]{3,2,1,0:T(8,128)(2,1)} async-done(((bf16[1,2,64,512]{3,2,1,0:T(8,128)(2,1)}), bf16[1,2,64,4096]{3,2,1,0:T(8,128)(2,1)}) %all-gather.9.cloned.1.call-update) | async-done | bytes 1048592 | tf_op jit(solution)/shard_map/all_gather | solution.py:40
  53.3 37.1 %all-gather.5.cloned.1.call-done = bf16[1,2,64,4096]{3,2,1,0:T(8,128)(2,1)} async-done(((bf16[1,2,64,512]{3,2,1,0:T(8,128)(2,1)}), bf16[1,2,64,4096]{3,2,1,0:T(8,128)(2,1)}) %all-gather.5.cloned.1.call-update) | async-done | bytes 1048592 | tf_op jit(solution)/shard_map/all_gather | solution.py:41
  92.2 2.4 gather_fusion.1
  94.6 2.4 gather_fusion
  97.0 4.6 %broadcast_select_fusion.1 = (bf16[40,128,256]{2,1,0:T(8,128)(2,1)S(1)}, bf16[40,128,256]{2,1,0:T(8,128)(2,1)}) fusion(bf16[40,128,256]{2,1,0:T(8,128)(2,1)} %gather_fusion, pred[40]{0:T(512)(128)(4,1)S(1)} %compare_and_fusion, bf16[40,128,256]{2,1,0:T(8,128)(2,1)} %gather_fusion.1), kind=kLoop, calls=%fused_computation.18 | loop fusion | flops 2621440 | bytes 10485800 | tf_op jit(solution)/shard_map/jit(_take)/select_n | solution.py:54
  101.6 30.2 %all-gather.7.cloned.1.call-done = bf16[256,8,5,256]{3,0,2,1:T(8,128)(2,1)} async-done(((bf16[16,8,5,256]{3,0,2,1:T(8,128)(2,1)}), bf16[256,8,5,256]{3,0,2,1:T(8,128)(2,1)}) %all-gather.7.cloned.1.call-update) | async-done | bytes 5242896 | tf_op jit(solution)/shard_map/all_gather | solution.py:37
  131.8 4.3 %fusion.9 = bf16[128,8,256]{2,0,1:T(8,128)(2,1)S(1)} fusion(bf16[128,8,5,256]{3,0,2,1:T(8,128)(2,1)S(1)} %bitcast.97, bf16[256,8,5,256]{3,0,2,1:T(8,128)(2,1)} %all-gather.7.cloned.1.call-done), kind=kOutput, calls=%fused_computation.39 | convolution fusion | flops 671350784 | bytes 8388608 | tf_op jit(solution)/shard_map/tckd,fckd->tcf/dot_general | solution.py:62
  138.6 2.1 collective-permute-start
  140.7 3.4 collective-permute-start.1
  144.2 2.0 collective-permute-done
  146.3 3.6 collective-permute-done.1
  152.2 25.9 %all-gather.11.cloned.1.call-done = bf16[256,8,5,256]{3,0,2,1:T(8,128)(2,1)} async-done(((bf16[16,8,5,256]{3,0,2,1:T(8,128)(2,1)}), bf16[256,8,5,256]{3,0,2,1:T(8,128)(2,1)}) %all-gather.11.cloned.1.call-update) | async-done | bytes 5242896 | tf_op jit(solution)/shard_map/all_gather | solution.py:36
  178.1 5.1 %multiply_convert_fusion = (bf16[128,8,256]{2,0,1:T(8,128)(2,1)S(1)}, bf16[128,8,256]{2,0,1:T(8,128)(2,1)}) fusion(f32[128,8,256]{2,1,0:T(8,128)} %bitcast.108, bf16[128,8,5,256]{3,0,2,1:T(8,128)(2,1)S(1)} %bitcast.99, bf16[256,8,5,256]{3,0,2,1:T(8,128)(2,1)} %all-gather.11.cloned.1.call-done), kind=kOutput, calls=%fused_computation.76 | convolution fusion | flops 676593664 | bytes 9961472 | tf_op jit(solution)/shard_map/tckb,bcke->tce/dot_general | solution.py:57
  184.4 2.1 reshape.189
  187.5 2.1 collective-permute-start.2
  189.7 3.6 collective-permute-start.3
  193.3 2.7 convolution_bitcast_fusion.1
  200.5 5.7 %fusion = bf16[256,2,8,5,256]{0,4,3,2,1:T(8,128)(2,1)} fusion(f32[256,1,8,5,256]{0,4,3,2,1:T(8,128)S(1)} %convolution_bitcast_fusion, f32[256,1,8,5,256]{0,4,3,2,1:T(8,128)S(1)} %convolution_bitcast_fusion.1), kind=kLoop, calls=%fused_computation.3 | loop fusion | flops 15728640 | bytes 31457280 | tf_op jit(solution)/shard_map/convert_element_type | solution.py:109
  206.2 15.4 %copy.56 = bf16[256,2,8,5,256]{4,2,3,1,0:T(8,128)(2,1)} copy(bf16[256,2,8,5,256]{0,4,3,2,1:T(8,128)(2,1)} %fusion) | data formatting | bytes 20971520 | tf_op jit(solution)/shard_map/convert_element_type | solution.py:109
  222.6 4.3 %convolution_bitcast_fusion.2 = f32[128,8,5,256]{3,0,2,1:T(8,128)S(1)} fusion(bf16[256,8,5,256]{3,0,2,1:T(8,128)(2,1)} %all-gather.11.cloned.1.call-done, bf16[128,8,256]{2,0,1:T(8,128)(2,1)S(1)} %copy-done.4), kind=kOutput, calls=%fused_computation.19 | convolution fusion | flops 671088640 | bytes 11010048 | tf_op jit(solution)/shard_map/tce,bcke->tckb/dot_general | solution.py:90
  227.0 5.9 %fusion.5 = bf16[128,16,256]{2,1,0:T(8,128)(2,1)} fusion(f32[128,8,5,256]{3,0,2,1:T(8,128)S(1)} %convolution_bitcast_fusion.2, s32[8,5]{0,1:T(8,128)S(1)} %copy.44), kind=kOutput, calls=%fused_computation.35 | convolution fusion | flops 252183168 | bytes 6291616 | tf_op jit(solution)/shard_map/tckb,ckr->trb/dot_general | solution.py:96
  232.8 2.3 convert_element_type.87
  236.4 117.1 %psum.7 = bf16[9,2048]{1,0:T(8,128)(2,1)S(1)} all-reduce(bf16[9,2048]{1,0:T(8,128)(2,1)S(1)} %multiply_convert_fusion.1), channel_id=1, replica_groups=mesh['crop'=2,'rows'=16,'hid'=8] {'crop','rows'}, use_global_device_ids=true, to_apply=%region_11.13 | all-reduce | flops 18432 | bytes 73728 | tf_op jit(solution)/shard_map/psum | solution.py:89
  356.1 17.5 %reduce-scatter.3.cloned.1.call-done = bf16[1,2,64,512]{3,2,1,0:T(8,128)(2,1)} async-done(((bf16[1,2,64,4096]{3,2,1,0:T(8,128)(2,1)}), bf16[1,2,64,512]{3,2,1,0:T(8,128)(2,1)}) %reduce-scatter.3.cloned.1.call-update) | async-done | bytes 131088 | tf_op jit(solution)/shard_map/reduce_scatter | solution.py:99
  (59 shorter events, 25.8 us)
Async XLA Ops:
  7.2 44.3 %all-gather.9.cloned.1.call-start = ((), (), s32[]{:S(2)}) async-start(), calls=%async_computation.4 | async-start | bytes 1179648 | tf_op jit(solution)/shard_map/all_gather | solution.py:40
  7.9 82.5 %all-gather.5.cloned.1.call-start = ((), (), s32[]{:S(2)}) async-start(), calls=%async_computation.2 | async-start | bytes 1179648 | tf_op jit(solution)/shard_map/all_gather | solution.py:41
  8.6 123.2 %all-gather.7.cloned.1.call-start = ((), (), s32[]{:S(2)}) async-start(), calls=%async_computation.3 | async-start | bytes 5570560 | tf_op jit(solution)/shard_map/all_gather | solution.py:37
  10.5 167.7 %all-gather.11.cloned.1.call-start = ((), (), s32[]{:S(2)}) async-start(), calls=%async_computation.5 | async-start | bytes 5570560 | tf_op jit(solution)/shard_map/all_gather | solution.py:36
  12.3 341.8 %reduce-scatter.5.cloned.1.call-start = ((), (), s32[]{:S(2)}) async-start(), calls=%async_computation.7 | async-start | bytes 10813440 | tf_op jit(solution)/shard_map/reduce_scatter | solution.py:108
  101.6 34.5 %copy-start = (bf16[40,128,256]{2,1,0:T(8,128)(2,1)}, bf16[40,128,256]{2,1,0:T(8,128)(2,1)S(1)}, u32[]{:S(2)}) copy-start(bf16[40,128,256]{2,1,0:T(8,128)(2,1)S(1)} %get-tuple-element.43) | copy-start | bytes 7864324
  136.1 8.0 %copy-start.5 = (f32[9,2048]{1,0:T(8,128)S(1)}, f32[9,2048]{1,0:T(8,128)}, u32[]{:S(2)}) copy-start(f32[9,2048]{1,0:T(8,128)} %param.12) | copy-start | bytes 221188
  138.6 7.7 %collective-permute-start = (bf16[1,1,64,2048]{3,2,1,0:T(8,128)(2,1)S(1)}, bf16[1,1,64,2048]{3,2,1,0:T(8,128)(2,1)S(1)}, u32[]{:S(2)}, u32[]{:S(2)}) collective-permute-start(bf16[1,1,64,2048]{3,2,1,0:T(8,128)(2,1)S(1)} %get-tuple-element.32), channel_id=1, source_target_pairs={{0,8},{8,16},{16,24},{24,32},{32,40},{40,48},{48,56},{56,64},{64,7... | collective-permute-start | bytes 786440 | tf_op jit(solution)/shard_map/ppermute | solution.py:18
  140.7 9.2 %collective-permute-start.1 = (bf16[1,1,64,2048]{3,2,1,0:T(8,128)(2,1)S(1)}, bf16[1,1,64,2048]{3,2,1,0:T(8,128)(2,1)S(1)}, u32[]{:S(2)}, u32[]{:S(2)}) collective-permute-start(bf16[1,1,64,2048]{3,2,1,0:T(8,128)(2,1)S(1)} %get-tuple-element.33), channel_id=1, source_target_pairs={{8,0},{16,8},{24,16},{32,24},{40,32},{48,40},{56,48},{64,56},{72,6... | collective-permute-start | bytes 786440 | tf_op jit(solution)/shard_map/ppermute | solution.py:19
  150.0 28.1 %copy-start.2 = (bf16[40,128,256]{2,1,0:T(8,128)(2,1)S(1)}, bf16[40,128,256]{2,1,0:T(8,128)(2,1)}, u32[]{:S(2)}) copy-start(bf16[40,128,256]{2,1,0:T(8,128)(2,1)} %get-tuple-element.44) | copy-start | bytes 7864324
  187.5 8.4 %collective-permute-start.2 = (bf16[1,1,64,2048]{3,2,1,0:T(8,128)(2,1)S(1)}, bf16[1,1,64,2048]{3,2,1,0:T(8,128)(2,1)S(1)}, u32[]{:S(2)}, u32[]{:S(2)}) collective-permute-start(bf16[1,1,64,2048]{3,2,1,0:T(8,128)(2,1)S(1)} %get-tuple-element.30), channel_id=1, source_target_pairs={{0,8},{8,16},{16,24},{24,32},{32,40},{40,48},{48,56},{56,64},{64,7... | collective-permute-start | bytes 786440 | tf_op jit(solution)/shard_map/ppermute | solution.py:18
  189.7 7.3 %collective-permute-start.3 = (bf16[1,1,64,2048]{3,2,1,0:T(8,128)(2,1)S(1)}, bf16[1,1,64,2048]{3,2,1,0:T(8,128)(2,1)S(1)}, u32[]{:S(2)}, u32[]{:S(2)}) collective-permute-start(bf16[1,1,64,2048]{3,2,1,0:T(8,128)(2,1)S(1)} %get-tuple-element.31), channel_id=1, source_target_pairs={{8,0},{16,8},{24,16},{32,24},{40,32},{48,40},{56,48},{64,56},{72,6... | collective-permute-start | bytes 786440 | tf_op jit(solution)/shard_map/ppermute | solution.py:19
  193.3 3.7 copy-start.3
  197.2 1.7 copy-start.1
  221.6 0.7 copy-start.6
  221.6 1.1 copy-start.4
  221.6 152.0 %reduce-scatter.3.cloned.1.call-start = ((), (), s32[]{:S(2)}) async-start(), calls=%async_computation.6 | async-start | bytes 1179648 | tf_op jit(solution)/shard_map/reduce_scatter | solution.py:99
Sparse Core Ops, SparseCore 0:
  9.8 41.6 all-gather.8
  53.3 37.0 all-gather.4
  92.8 39.0 all-gather.6
  134.0 44.0 all-gather.10
  221.7 110.2 reduce-scatter.4
  335.1 38.3 reduce-scatter.2
where the time goes:
time: 381 us; the launch traced here: 380 us
  waiting for transfers between devices  157 us (41%)
  blocking collectives  117 us (31%)
  local copies, waits for them, and re-layouts  41.1 us (11%)
  matrix products  23.8 us (6%)
  other arithmetic  15.2 us (4%)
  between operations  14.3 us (4%)
  starting transfers between devices  11.8 us (3%)
    psum x1, blocking collectives, on_device(): lax.psum(kern_local.astype(jnp.bfloat16), ('crop', 'rows'))  117 us
    all_gather x1, waiting for transfers between devices, on_device(): lax.all_gather(tokens, 'hid', axis=3, tiled=True)  38.3 us
    all_gather x1, waiting for transfers between devices, on_device(): lax.all_gather(cotangent, 'hid', axis=3, tiled=True)  37.1 us
    all_gather x1, waiting for transfers between devices, on_device(): lax.all_gather(weight_out, 'rows', axis=0, tiled=True)  30.2 us
    all_gather x1, waiting for transfers between devices, on_device(): lax.all_gather(weight_in, 'rows', axis=0, tiled=True)  25.9 us
    reduce_scatter x1, waiting for transfers between devices, on_device(): lax.psum_scatter(token_terms.astype(jnp.bfloat16), 'hid', scatter_dimensi...  17.5 us
    convert_element_type x1, local copies, waits for them, and re-layouts, on_device(): (jnp.stack([first_term, second_term], axis=1) * loss_scale).astype(jnp.bf...  15.4 us
    unnamed x21, local copies, waits for them, and re-layouts  9.42 us
  transfers between devices with their start and end apart: 10, of which 8 were waited for; matrix products, arithmetic and copies ran while one was open for 12% of the time, Pallas kernels for 0%

commit v1 on v0

--- a/solution.py
+++ b/solution.py
@@ -86,7 +86,9 @@
     kern_local = jnp.stack(kern_terms, axis=0) * loss_scale
     mix_out = mix_sum.astype(jnp.bfloat16).reshape(tok_count, col_count, block_size)
     pre_grad = (act_grad.reshape(tok_count, col_count, block_size) * slopes).astype(jnp.bfloat16)
-    kern_total = lax.psum(kern_local.astype(jnp.bfloat16), ("crop", "rows")).astype(jnp.float32)
+    kern_total = jnp.sum(
+        lax.all_gather(kern_local.astype(jnp.bfloat16), ("crop", "rows")), axis=0
+    ).astype(jnp.float32)
     back_select = jnp.einsum(
         "tce,bcke->tckb", pre_grad, in_panel, preferred_element_type=jnp.float32
     )

time: 381 us -> 407 us (1.068)
  waiting for transfers between devices: 157 us -> 303 us
  blocking collectives: 117 us -> 0 us
  local copies, waits for them, and re-layouts: 41.1 us -> 36.4 us
    psum x1 -> x0, blocking collectives: 117 us -> none  [on_device(): lax.psum(kern_local.astype(jnp.bfloat16), ('crop', 'rows'))]
    reduce_scatter x1, waiting for transfers between devices: 0.01 us -> 107 us  [on_device(): lax.psum_scatter((jnp.stack([first_term, second_term], axis=1) * loss_sca...]
    reduce_scatter x1, waiting for transfers between devices: 17.5 us -> 39.8 us  [on_device(): lax.psum_scatter(token_terms.astype(jnp.bfloat16), 'hid', scatter_dimensi...]
    all_gather x0 -> x1, waiting for transfers between devices: none -> 13.9 us  [on_device(): lax.all_gather(kern_local.astype(jnp.bfloat16), ('crop', 'rows'))]
    unnamed x21 -> x19, local copies, waits for them, and re-layouts: 9.42 us -> 9.33 us
  transfers between devices with their start and end apart: 10 -> 11, of which waited for: 8 -> 11; matrix products, arithmetic and copies ran while one was open for 12% -> 17% of each run, Pallas kernels for 0% -> 0%
where the time goes in v1:
time: 407 us; the launch traced here: 406 us
  waiting for transfers between devices  303 us (74%)
  local copies, waits for them, and re-layouts  36.4 us (9%)
  matrix products  23.5 us (6%)
  other arithmetic  17.8 us (4%)
  between operations  14.4 us (4%)
  starting transfers between devices  11.6 us (3%)
    reduce_scatter x1, waiting for transfers between devices, on_device(): lax.psum_scatter((jnp.stack([first_term, second_term], axis=1) * loss_sca...  107 us
    reduce_scatter x1, waiting for transfers between devices, on_device(): lax.psum_scatter(token_terms.astype(jnp.bfloat16), 'hid', scatter_dimensi...  39.8 us
    all_gather x1, waiting for transfers between devices, on_device(): lax.all_gather(tokens, 'hid', axis=3, tiled=True)  38.3 us
    all_gather x1, waiting for transfers between devices, on_device(): lax.all_gather(cotangent, 'hid', axis=3, tiled=True)  37.1 us
    all_gather x1, waiting for transfers between devices, on_device(): lax.all_gather(weight_out, 'rows', axis=0, tiled=True)  30.2 us
    all_gather x1, waiting for transfers between devices, on_device(): lax.all_gather(weight_in, 'rows', axis=0, tiled=True)  25.9 us
    convert_element_type x1, local copies, waits for them, and re-layouts, on_device(): (jnp.stack([first_term, second_term], axis=1) * loss_scale).astype(jnp.bf...  15.5 us
    all_gather x1, waiting for transfers between devices, on_device(): lax.all_gather(kern_local.astype(jnp.bfloat16), ('crop', 'rows'))  13.9 us
  transfers between devices with their start and end apart: 11, of which 11 were waited for; matrix products, arithmetic and copies ran while one was open for 17% of the time, Pallas kernels for 0%

profile of v1, /device:TPU:4, one launch (start us, length us, event | category | flops | bytes accessed | tf_op | source)
XLA Modules:
  0.0 406.3 jit_solution(9515083838924378157)
XLA Ops:
  13.2 38.3 %all-gather.10.cloned.1.call-done = bf16[1,2,64,4096]{3,2,1,0:T(8,128)(2,1)} async-done(((bf16[1,2,64,512]{3,2,1,0:T(8,128)(2,1)}), bf16[1,2,64,4096]{3,2,1,0:T(8,128)(2,1)}) %all-gather.10.cloned.1.call-update) | async-done | bytes 1048592 | tf_op jit(solution)/shard_map/all_gather | solution.py:40
  53.3 37.1 %all-gather.6.cloned.1.call-done = bf16[1,2,64,4096]{3,2,1,0:T(8,128)(2,1)} async-done(((bf16[1,2,64,512]{3,2,1,0:T(8,128)(2,1)}), bf16[1,2,64,4096]{3,2,1,0:T(8,128)(2,1)}) %all-gather.6.cloned.1.call-update) | async-done | bytes 1048592 | tf_op jit(solution)/shard_map/all_gather | solution.py:41
  92.2 2.4 gather_fusion.1
  94.6 2.4 gather_fusion
  97.0 4.6 %broadcast_select_fusion.1 = (bf16[40,128,256]{2,1,0:T(8,128)(2,1)S(1)}, bf16[40,128,256]{2,1,0:T(8,128)(2,1)}) fusion(bf16[40,128,256]{2,1,0:T(8,128)(2,1)} %gather_fusion, pred[40]{0:T(512)(128)(4,1)S(1)} %compare_and_fusion, bf16[40,128,256]{2,1,0:T(8,128)(2,1)} %gather_fusion.1), kind=kLoop, calls=%fused_computation.18 | loop fusion | flops 2621440 | bytes 10485800 | tf_op jit(solution)/shard_map/jit(_take)/select_n | solution.py:54
  101.6 30.2 %all-gather.8.cloned.1.call-done = bf16[256,8,5,256]{3,0,2,1:T(8,128)(2,1)} async-done(((bf16[16,8,5,256]{3,0,2,1:T(8,128)(2,1)}), bf16[256,8,5,256]{3,0,2,1:T(8,128)(2,1)}) %all-gather.8.cloned.1.call-update) | async-done | bytes 5242896 | tf_op jit(solution)/shard_map/all_gather | solution.py:37
  131.8 4.3 %fusion.9 = bf16[128,8,256]{2,0,1:T(8,128)(2,1)S(1)} fusion(bf16[128,8,5,256]{3,0,2,1:T(8,128)(2,1)S(1)} %bitcast.97, bf16[256,8,5,256]{3,0,2,1:T(8,128)(2,1)} %all-gather.8.cloned.1.call-done), kind=kOutput, calls=%fused_computation.39 | convolution fusion | flops 671350784 | bytes 8388608 | tf_op jit(solution)/shard_map/tckd,fckd->tcf/dot_general | solution.py:62
  138.6 2.1 collective-permute-start
  140.7 3.4 collective-permute-start.1
  144.2 2.0 collective-permute-done
  146.3 3.6 collective-permute-done.1
  152.2 25.9 %all-gather.12.cloned.1.call-done = bf16[256,8,5,256]{3,0,2,1:T(8,128)(2,1)} async-done(((bf16[16,8,5,256]{3,0,2,1:T(8,128)(2,1)}), bf16[256,8,5,256]{3,0,2,1:T(8,128)(2,1)}) %all-gather.12.cloned.1.call-update) | async-done | bytes 5242896 | tf_op jit(solution)/shard_map/all_gather | solution.py:36
  178.1 5.1 %multiply_convert_fusion = (bf16[128,8,256]{2,0,1:T(8,128)(2,1)S(1)}, bf16[128,8,256]{2,0,1:T(8,128)(2,1)}) fusion(f32[128,8,256]{2,1,0:T(8,128)} %bitcast.108, bf16[128,8,5,256]{3,0,2,1:T(8,128)(2,1)S(1)} %bitcast.100, bf16[256,8,5,256]{3,0,2,1:T(8,128)(2,1)} %all-gather.12.cloned.1.call-done), kind=kOutput, calls=%fused_computation.76 | convolution fusion | flops 676593664 | bytes 9961472 | tf_op jit(solution)/shard_map/tckb,bcke->tce/dot_general | solution.py:57
  183.9 2.1 collective-permute-start.2
  186.0 3.4 collective-permute-start.3
  189.5 2.1 collective-permute-done.2
  195.6 3.3 convolution_bitcast_fusion.1
  202.2 5.7 %fusion = bf16[256,2,8,5,256]{0,4,3,2,1:T(8,128)(2,1)} fusion(f32[256,1,8,5,256]{0,4,3,2,1:T(8,128)S(1)} %convolution_bitcast_fusion, f32[256,1,8,5,256]{0,4,3,2,1:T(8,128)S(1)} %convolution_bitcast_fusion.1), kind=kLoop, calls=%fused_computation.3 | loop fusion | flops 15728640 | bytes 31457280 | tf_op jit(solution)/shard_map/convert_element_type | solution.py:111
  207.9 15.5 %copy.56 = bf16[256,2,8,5,256]{4,2,3,1,0:T(8,128)(2,1)} copy(bf16[256,2,8,5,256]{0,4,3,2,1:T(8,128)(2,1)} %fusion) | data formatting | bytes 20971520 | tf_op jit(solution)/shard_map/convert_element_type | solution.py:111
  224.2 4.3 %convolution_bitcast_fusion.2 = f32[128,8,5,256]{3,0,2,1:T(8,128)S(1)} fusion(bf16[256,8,5,256]{3,0,2,1:T(8,128)(2,1)} %all-gather.12.cloned.1.call-done, bf16[128,8,256]{2,0,1:T(8,128)(2,1)S(1)} %copy-done.3), kind=kOutput, calls=%fused_computation.19 | convolution fusion | flops 671088640 | bytes 11010048 | tf_op jit(solution)/shard_map/tce,bcke->tckb/dot_general | solution.py:92
  228.5 4.9 %fusion.5 = bf16[128,16,256]{2,1,0:T(8,128)(2,1)S(1)} fusion(f32[128,8,5,256]{3,0,2,1:T(8,128)S(1)} %convolution_bitcast_fusion.2, s32[8,5]{0,1:T(8,128)S(1)} %copy.44), kind=kOutput, calls=%fused_computation.35 | convolution fusion | flops 252183168 | bytes 6291616 | tf_op jit(solution)/shard_map/tckb,ckr->trb/dot_general | solution.py:98
  234.7 13.9 %all-gather.14.cloned.1.call-done = bf16[32,9,2048]{2,1,0:T(8,128)(2,1)} async-done(((bf16[1,9,2048]{2,1,0:T(8,128)(2,1)}), bf16[32,9,2048]{2,1,0:T(8,128)(2,1)}) %all-gather.14.cloned.1.call-update) | async-done | bytes 1179664 | tf_op jit(solution)/shard_map/all_gather | solution.py:90
  251.2 106.5 %reduce-scatter.5.cloned.1.call-done = bf16[8,2,8,5,256]{4,2,3,1,0:T(8,128)(2,1)} async-done(((bf16[256,2,8,5,256]{4,2,3,1,0:T(8,128)(2,1)}), bf16[8,2,8,5,256]{4,2,3,1,0:T(8,128)(2,1)}) %reduce-scatter.5.cloned.1.call-update) | async-done | bytes 327696 | tf_op jit(solution)/shard_map/reduce_scatter | solution.py:110
  359.6 39.8 %reduce-scatter.3.cloned.1.call-done = bf16[1,2,64,512]{3,2,1,0:T(8,128)(2,1)} async-done(((bf16[1,2,64,4096]{3,2,1,0:T(8,128)(2,1)}), bf16[1,2,64,512]{3,2,1,0:T(8,128)(2,1)}) %reduce-scatter.3.cloned.1.call-update) | async-done | bytes 131088 | tf_op jit(solution)/shard_map/reduce_scatter | solution.py:101
  (60 shorter events, 28.8 us)
Async XLA Ops:
  7.2 44.3 %all-gather.10.cloned.1.call-start = ((), (), s32[]{:S(2)}) async-start(), calls=%async_computation.4 | async-start | bytes 1179648 | tf_op jit(solution)/shard_map/all_gather | solution.py:40
  7.9 82.5 %all-gather.6.cloned.1.call-start = ((), (), s32[]{:S(2)}) async-start(), calls=%async_computation.2 | async-start | bytes 1179648 | tf_op jit(solution)/shard_map/all_gather | solution.py:41
  8.6 123.2 %all-gather.8.cloned.1.call-start = ((), (), s32[]{:S(2)}) async-start(), calls=%async_computation.3 | async-start | bytes 5570560 | tf_op jit(solution)/shard_map/all_gather | solution.py:37
  10.5 167.7 %all-gather.12.cloned.1.call-start = ((), (), s32[]{:S(2)}) async-start(), calls=%async_computation.5 | async-start | bytes 5570560 | tf_op jit(solution)/shard_map/all_gather | solution.py:36
  12.3 236.3 %all-gather.14.cloned.1.call-start = ((), (), s32[]{:S(2)}) async-start(), calls=%async_computation.8 | async-start | bytes 2162688 | tf_op jit(solution)/shard_map/all_gather | solution.py:90
  101.6 34.5 %copy-start = (bf16[40,128,256]{2,1,0:T(8,128)(2,1)}, bf16[40,128,256]{2,1,0:T(8,128)(2,1)S(1)}, u32[]{:S(2)}) copy-start(bf16[40,128,256]{2,1,0:T(8,128)(2,1)S(1)} %get-tuple-element.43) | copy-start | bytes 7864324
  136.1 8.0 %copy-start.4 = (f32[9,2048]{1,0:T(8,128)S(1)}, f32[9,2048]{1,0:T(8,128)}, u32[]{:S(2)}) copy-start(f32[9,2048]{1,0:T(8,128)} %param.12) | copy-start | bytes 221188
  138.6 7.7 %collective-permute-start = (bf16[1,1,64,2048]{3,2,1,0:T(8,128)(2,1)S(1)}, bf16[1,1,64,2048]{3,2,1,0:T(8,128)(2,1)S(1)}, u32[]{:S(2)}, u32[]{:S(2)}) collective-permute-start(bf16[1,1,64,2048]{3,2,1,0:T(8,128)(2,1)S(1)} %get-tuple-element.32), channel_id=1, source_target_pairs={{0,8},{8,16},{16,24},{24,32},{32,40},{40,48},{48,56},{56,64},{64,7... | collective-permute-start | bytes 786440 | tf_op jit(solution)/shard_map/ppermute | solution.py:18
  140.7 9.2 %collective-permute-start.1 = (bf16[1,1,64,2048]{3,2,1,0:T(8,128)(2,1)S(1)}, bf16[1,1,64,2048]{3,2,1,0:T(8,128)(2,1)S(1)}, u32[]{:S(2)}, u32[]{:S(2)}) collective-permute-start(bf16[1,1,64,2048]{3,2,1,0:T(8,128)(2,1)S(1)} %get-tuple-element.33), channel_id=1, source_target_pairs={{8,0},{16,8},{24,16},{32,24},{40,32},{48,40},{56,48},{64,56},{72,6... | collective-permute-start | bytes 786440 | tf_op jit(solution)/shard_map/ppermute | solution.py:19
  150.1 28.1 %copy-start.2 = (bf16[40,128,256]{2,1,0:T(8,128)(2,1)S(1)}, bf16[40,128,256]{2,1,0:T(8,128)(2,1)}, u32[]{:S(2)}) copy-start(bf16[40,128,256]{2,1,0:T(8,128)(2,1)} %get-tuple-element.44) | copy-start | bytes 7864324
  183.9 7.7 %collective-permute-start.2 = (bf16[1,1,64,2048]{3,2,1,0:T(8,128)(2,1)S(1)}, bf16[1,1,64,2048]{3,2,1,0:T(8,128)(2,1)S(1)}, u32[]{:S(2)}, u32[]{:S(2)}) collective-permute-start(bf16[1,1,64,2048]{3,2,1,0:T(8,128)(2,1)S(1)} %get-tuple-element.30), channel_id=1, source_target_pairs={{0,8},{8,16},{16,24},{24,32},{32,40},{40,48},{48,56},{56,64},{64,7... | collective-permute-start | bytes 786440 | tf_op jit(solution)/shard_map/ppermute | solution.py:18
  186.0 7.3 %collective-permute-start.3 = (bf16[1,1,64,2048]{3,2,1,0:T(8,128)(2,1)S(1)}, bf16[1,1,64,2048]{3,2,1,0:T(8,128)(2,1)S(1)}, u32[]{:S(2)}, u32[]{:S(2)}) collective-permute-start(bf16[1,1,64,2048]{3,2,1,0:T(8,128)(2,1)S(1)} %get-tuple-element.31), channel_id=1, source_target_pairs={{8,0},{16,8},{24,16},{32,24},{40,32},{48,40},{56,48},{64,56},{72,6... | collective-permute-start | bytes 786440 | tf_op jit(solution)/shard_map/ppermute | solution.py:19
  193.5 2.1 copy-start.3
  195.3 162.4 %reduce-scatter.5.cloned.1.call-start = ((), (), s32[]{:S(2)}) async-start(), calls=%async_computation.7 | async-start | bytes 10813440 | tf_op jit(solution)/shard_map/reduce_scatter | solution.py:110
  198.9 1.7 copy-start.1
  223.4 0.7 copy-start.5
  223.4 176.0 %reduce-scatter.3.cloned.1.call-start = ((), (), s32[]{:S(2)}) async-start(), calls=%async_computation.6 | async-start | bytes 1179648 | tf_op jit(solution)/shard_map/reduce_scatter | solution.py:101
Sparse Core Ops, SparseCore 0:
  9.8 41.6 all-gather.9
  53.3 37.0 all-gather.5
  92.8 39.0 all-gather.7
  134.0 44.0 all-gather.11
  195.5 53.0 all-gather.13
  252.5 105.1 reduce-scatter.4
  361.0 38.3 reduce-scatter.2
